TPU v7x, 32 devices: a whole 2x2x4 slice. The times are simulated.
32 devices in a mesh: groups: 2 (over y), space: 4 (over x, core), chan: 4 (over z).
Axes of the slice: x: 2, y: 2, z: 4, core: 2. Of those that a mesh axis runs over, the one named last changes fastest.
Arguments:
- volume: bfloat16 [32, 16, 256, 256], P(('groups', 'space'), 'chan'), parts along dimension 0, may hold values from -6 to 6
- weight: bfloat16 [8, 256, 256], P(None, 'space', 'chan'), may hold values from -0.125 to 0.125
- cotangent: bfloat16 [16, 8, 128, 256], P(('groups', 'space'), None, None, 'chan'), parts along dimension 0, may hold values from -6 to 6
Outputs:
- grad_volume: bfloat16 [32, 16, 256, 256], P(('groups', 'space'), 'chan'), parts along dimension 0
- grad_weight: float32 [16, 256, 256], P('groups', 'space', 'chan'), parts along dimension 0
There are 2 independent parts, one for each index of `groups`. A program takes and returns all parts, laid end to end along the dimension named above; an argument that names none is the same for every part. Nothing has to cross between parts.
All inputs are finite; a program needn't handle non-finite values.
Results may differ from a plain program's by a relative error of at most 0.0049.
Values may be sent and summed in bfloat16 or wider, within the bound.
A program may use at most 64 MiB of HBM per device.

v0:
```python
import jax
import jax.numpy as jnp
from jax import lax
from jax.sharding import PartitionSpec as P


def patch_rows(block):
    cells_x, cells_y, cells_z, in_chan = block.shape
    shaped = block.reshape(cells_x // 2, 2, cells_y // 2, 2, cells_z // 2, 2, in_chan)
    return shaped.transpose(0, 2, 4, 1, 3, 5, 6).reshape(-1, 8, in_chan)


def unpatch(rows, cells_x, cells_y, cells_z):
    in_chan = rows.shape[2]
    shaped = rows.reshape(cells_x // 2, cells_y // 2, cells_z // 2, 2, 2, 2, in_chan)
    return shaped.transpose(0, 3, 1, 4, 2, 5, 6).reshape(cells_x, cells_y, cells_z, in_chan)


def shards(volume, weight, cotangent):
    cells_x, cells_y, cells_z, in_chan = volume.shape
    patches = patch_rows(volume)
    out_rows = patches.shape[0]
    wide_w = lax.all_gather(weight, "chan", axis=2, tiled=True)
    cot_tiles = lax.all_to_all(cotangent, "chan", split_axis=1, concat_axis=3, tiled=True)
    out_chan = cot_tiles.shape[3]
    upstream = cot_tiles.reshape(out_rows, out_chan)
    whole_w = lax.all_gather(wide_w, "space", axis=1, tiled=True)
    pre_act = jnp.einsum("mkc,kco->mo", patches, whole_w, preferred_element_type=jnp.float32)
    squash = jax.nn.sigmoid(pre_act)
    slopes = squash * (1.0 + pre_act * (1.0 - squash))
    deltas = (upstream.astype(jnp.float32) * slopes).astype(jnp.bfloat16)
    grad_rows = jnp.einsum(
        "mo,kco->mkc", deltas, whole_w, preferred_element_type=jnp.float32
    ).astype(jnp.bfloat16)
    grad_volume = unpatch(grad_rows, cells_x, cells_y, cells_z)
    partial_w = jnp.einsum("mkc,mo->kco", patches, deltas, preferred_element_type=jnp.float32)
    by_chan = lax.psum_scatter(partial_w, "chan", scatter_dimension=2, tiled=True)
    owned_sum = lax.psum_scatter(by_chan, "space", scatter_dimension=1, tiled=True)
    grad_weight = owned_sum / out_rows
    return (grad_volume, grad_weight)


def solution(mesh):
    return jax.shard_map(
        shards,
        mesh=mesh,
        in_specs=(
            P(("groups", "space"), "chan", None, None),
            P(None, "space", "chan"),
            P(("groups", "space"), None, None, "chan"),
        ),
        out_specs=(P(("groups", "space"), "chan", None, None), P("groups", "space", "chan")),
        check_vma=False,
    )
```

profile of v0, /device:TPU:0, one launch (start us, length us, event | category | flops | bytes accessed | tf_op | source)
XLA Modules:
  0.0 125.6 jit_solution(15146380185082460627)
XLA Ops:
  7.2 0.0 copy-start.2
  7.2 0.0 copy-start
  7.2 0.0 all-gather.2.cloned.1.call-start
  7.2 1.2 copy.19
  8.4 17.4 %all_gather.6 = bf16[8,64,256]{1,0,2:T(8,128)(2,1)S(1)} all-gather(bf16[8,64,64]{1,0,2:T(8,128)(2,1)S(1)} %copy.19), channel_id=1, replica_groups=mesh['groups'=2,'space'=4,'chan'=4] {'chan'}, dimensions={2}, use_global_device_ids=true | all-gather | bytes 327680 | tf_op jit(solution)/shard_map/all_gather | solution.py:23
  25.8 1.0 copy.20
  26.8 0.0 all-gather.2.cloned.1.call-update
  26.9 0.0 copy-done.2
  26.9 0.7 copy.16
  27.6 5.4 %all-to-all-start = ((bf16[2,8,128,64]{2,3,0,1:T(8,128)(2,1)}), bf16[2,8,128,64]{2,3,0,1:T(8,128)(2,1)S(1)}, u32[]{:S(2)}, u32[]{:S(2)}) async-start(bf16[2,8,128,64]{2,3,0,1:T(8,128)(2,1)} %copy.16), calls=%async_computation | async-start | bytes 524288 | tf_op jit(solution)/shard_map/all_to_all | solution.py:24
  33.0 0.0 reduce-scatter.5.cloned.1.call-start
  33.0 0.0 copy-done
  33.0 2.2 %reshape.22 = bf16[2,2,2,2,128,2,256]{6,5,4,3,2,1,0:T(2,128)(2,1)} reshape(bf16[4,4,256,256]{3,2,1,0:T(8,128)(2,1)S(1)} %copy-done) | data formatting | bytes 4194304 | tf_op jit(solution)/shard_map/reshape | solution.py:9
  35.2 2.1 %copy.18 = bf16[2,2,128,2,2,2,256]{6,2,1,0,5,4,3:T(8,128)(2,1)S(1)} copy(bf16[2,2,128,2,2,2,256]{6,5,2,4,1,3,0:T(2,128)(2,1)} %bitcast.37) | data formatting | bytes 4194304 | tf_op jit(solution)/shard_map/transpose | solution.py:10
  37.3 2.4 %all-to-all-done = bf16[2,8,128,64]{2,3,0,1:T(8,128)(2,1)S(1)} async-done(((bf16[2,8,128,64]{2,3,0,1:T(8,128)(2,1)}), bf16[2,8,128,64]{2,3,0,1:T(8,128)(2,1)S(1)}, u32[]{:S(2)}, u32[]{:S(2)}) %all-to-all-start) | async-done | bytes 262176 | tf_op jit(solution)/shard_map/all_to_all | solution.py:24
  39.8 0.3 copy.30
  40.0 0.4 reshape.26
  40.5 1.0 copy.21
  41.4 4.0 %all-gather.2.cloned.1.call-done = bf16[8,256,256]{2,1,0:T(8,128)(2,1)} async-done(((bf16[8,64,256]{2,1,0:T(8,128)(2,1)}), bf16[8,256,256]{2,1,0:T(8,128)(2,1)}) %all-gather.2.cloned.1.call-update) | async-done | bytes 1048592 | tf_op jit(solution)/shard_map/all_gather | solution.py:27
  45.5 2.1 %fusion = bf16[512,256,1]{1,0,2:T(8,128)(2,1)S(1)} fusion(f32[512,256]{1,0:T(8,128)} %copy.21, bf16[512,8,256]{2,0,1:T(8,128)(2,1)S(1)} %bitcast.34, bf16[8,256,256]{2,1,0:T(8,128)(2,1)} %all-gather.2.cloned.1.call-done), kind=kOutput, calls=%fused_computation.5 | convolution fusion | flops 538050560 | bytes 3932160 | tf_op jit(solution)/shard_map/mkc,kco->mo/dot_general | solution.py:28
  47.6 2.0 %convolution_bitcast_fusion = f32[8,256,256]{1,2,0:T(8,128)} fusion(bf16[512,256,1]{1,0,2:T(8,128)(2,1)S(1)} %fusion, bf16[512,8,256]{2,0,1:T(8,128)(2,1)S(1)} %bitcast.35), kind=kOutput, calls=%fused_computation.1 | convolution fusion | flops 536870912 | bytes 4456448 | tf_op jit(solution)/shard_map/mkc,mo->kco/dot_general | solution.py:36
  49.7 0.0 reduce-scatter.5.cloned.1.call-update
  49.7 0.0 copy-start.1
  49.7 0.0 reduce-scatter.7.cloned.1.call-start
  49.7 43.7 %reduce-scatter.5.cloned.1.call-done = f32[8,256,64]{1,2,0:T(8,128)} async-done(((f32[8,256,256]{1,2,0:T(8,128)}), f32[8,256,64]{1,2,0:T(8,128)}) %reduce-scatter.5.cloned.1.call-update) | async-done | bytes 524304 | tf_op jit(solution)/shard_map/reduce_scatter | solution.py:37
  93.5 1.5 %copy.27 = f32[8,256,64]{2,0,1:T(8,128)S(1)} copy(f32[8,256,64]{1,2,0:T(8,128)} %reduce-scatter.5.cloned.1.call-done) | data formatting | bytes 1048576
  95.0 1.1 reshape.31
  96.0 0.0 reduce-scatter.7.cloned.1.call-update
  96.1 0.0 copy-done.1
  96.1 0.7 convolution_convert_fusion
  96.8 2.2 %copy.22 = bf16[2,2,2,2,128,2,256]{6,5,4,3,2,1,0:T(2,128)(2,1)S(1)} copy(bf16[2,2,2,2,128,2,256]{6,4,2,0,5,3,1:T(8,128)(2,1)S(1)} %bitcast.36) | data formatting | bytes 4194304 | tf_op jit(solution)/shard_map/transpose | solution.py:16
  99.0 2.2 %reshape.25 = bf16[4,4,256,256]{3,2,1,0:T(8,128)(2,1)} reshape(bf16[2,2,2,2,128,2,256]{6,5,4,3,2,1,0:T(2,128)(2,1)S(1)} %copy.22) | data formatting | bytes 4194304 | tf_op jit(solution)/shard_map/reshape | solution.py:16
  101.2 15.9 %reduce-scatter.7.cloned.1.call-done = f32[64,512]{1,0:T(8,128)} async-done(((f32[256,512]{1,0:T(8,128)}), f32[64,512]{1,0:T(8,128)}) %reduce-scatter.7.cloned.1.call-update) | async-done | bytes 131088
  117.1 1.0 reshape.32
  118.1 0.1 copy.28
  118.2 0.8 copy.24
  (1 shorter events, 0.0 us)
Async XLA Ops:
  7.2 19.7 %copy-start.2 = (bf16[2,8,128,64]{2,3,1,0:T(8,128)(2,1)S(1)}, bf16[2,8,128,64]{2,3,1,0:T(8,128)(2,1)}, u32[]{:S(2)}) copy-start(bf16[2,8,128,64]{2,3,1,0:T(8,128)(2,1)} %param.5) | copy-start | bytes 786436
  7.2 25.8 %copy-start = (bf16[4,4,256,256]{3,2,1,0:T(8,128)(2,1)S(1)}, bf16[4,4,256,256]{3,2,1,0:T(8,128)(2,1)}, u32[]{:S(2)}) copy-start(bf16[4,4,256,256]{3,2,1,0:T(8,128)(2,1)} %param.3) | copy-start | bytes 6291460
  7.2 38.3 %all-gather.2.cloned.1.call-start = ((), (), s32[]{:S(2)}) async-start(), calls=%async_computation.3 | async-start | bytes 1310720 | tf_op jit(solution)/shard_map/all_gather | solution.py:27
  27.6 12.2 %all-to-all-start = ((bf16[2,8,128,64]{2,3,0,1:T(8,128)(2,1)}), bf16[2,8,128,64]{2,3,0,1:T(8,128)(2,1)S(1)}, u32[]{:S(2)}, u32[]{:S(2)}) async-start(bf16[2,8,128,64]{2,3,0,1:T(8,128)(2,1)} %copy.16), calls=%async_computation | async-start | bytes 524288 | tf_op jit(solution)/shard_map/all_to_all | solution.py:24
  33.0 60.5 %reduce-scatter.5.cloned.1.call-start = ((), (), s32[]{:S(2)}) async-start(), calls=%async_computation.4 | async-start | bytes 2621440 | tf_op jit(solution)/shard_map/reduce_scatter | solution.py:37
  49.7 46.4 %copy-start.1 = (bf16[8,256,256]{2,1,0:T(8,128)(2,1)S(1)}, bf16[8,256,256]{2,1,0:T(8,128)(2,1)}, u32[]{:S(2)}) copy-start(bf16[8,256,256]{2,1,0:T(8,128)(2,1)} %all-gather.2.cloned.1.call-done) | copy-start | bytes 3145732
  49.7 67.4 %reduce-scatter.7.cloned.1.call-start = ((), (), s32[]{:S(2)}) async-start(), calls=%async_computation.5 | async-start | bytes 655360
Sparse Core Ops, SparseCore 0:
  27.0 18.4 all-gather.1
  49.8 43.6 reduce-scatter.4
  96.2 20.8 reduce-scatter.6
where the time goes:
time: 126 us
  waiting for transfers between devices  66.1 us (52%)
  local copies, waits for them, and re-layouts  17.9 us (14%)
  blocking collectives  17.4 us (14%)
  between operations  13.9 us (11%)
  starting transfers between devices  5.47 us (4%)
  matrix products  4.93 us (4%)
    reduce_scatter x1, waiting for transfers between devices, shards(): lax.psum_scatter(partial_w, 'chan', scatter_dimension=2, tiled=True)  43.7 us
    all_gather x1, blocking collectives, shards(): wide_w = lax.all_gather(weight, 'chan', axis=2, tiled=True)  17.4 us
    unnamed x4, waiting for transfers between devices  15.9 us
    unnamed x13, local copies, waits for them, and re-layouts  6.45 us
    all_to_all x1, starting transfers between devices, shards(): lax.all_to_all(cotangent, 'chan', split_axis=1, concat_axis=3, tiled=True)  5.38 us
    all_gather x1, waiting for transfers between devices, shards(): whole_w = lax.all_gather(wide_w, 'space', axis=1, tiled=True)  4.02 us
  transfers between devices with their start and end apart: 4, of which 4 were waited for; matrix products, arithmetic and copies ran while one was open for 9% of the time, Pallas kernels for 0%

commit v1 on v0

v1 whole, which is shorter than its diff:
```python
import functools

import jax
import jax.numpy as jnp
from jax import lax
from jax.experimental import pallas as pl
from jax.experimental.pallas import tpu as pltpu
from jax.sharding import PartitionSpec as P

MESH = pl.DeviceIdType.MESH
LANES = 128
BF = jnp.bfloat16
F32 = jnp.float32


def kernel(
    ns, nc, vol_hbm, w_ref, cot_ref, gv_hbm, gw_ref,
    vbuf, tmp, rows, cols, wpack, wfull, cot_out, cot_in, dlt, obuf,
    part, a_out, a_in, b_out, b_in, own, c_out, c_in,
    v_sem, o_sem, zs, zr, xs, xr, ks, kr, ts, tr, as_, ar, bs, br, cs, cr,
):
    nx = ns // 2
    ax, ay, nz, cin = vbuf.shape
    ci, oc = w_ref.shape[1:]
    pk = LANES // oc
    ng = 8 // pk
    half_i, half_j, half_l = ax // 2, ay // 2, nz // 2
    cells = half_i * half_j * half_l
    short = cells // pk
    halves = cin // LANES

    s, c = lax.axis_index("space"), lax.axis_index("chan")
    x, core = lax.div(s, 2), lax.rem(s, 2)
    other = 1 - core

    def c_at(d):
        return lax.rem(c + d, nc)

    def c_from(d):
        return lax.rem(c + nc - d, nc)

    def x_at(d):
        return lax.rem(x + d, nx)

    def x_from(d):
        return lax.rem(x + nx - d, nx)

    def to_z(d):
        return {"chan": c_at(d)}

    def to_x(d):
        return {"space": x_at(d) * 2 + core}

    partner = {"space": x * 2 + other}
    sent = []

    def send(src, dst, ssem, rsem, device):
        copy = pltpu.make_async_remote_copy(
            src_ref=src, dst_ref=dst, send_sem=ssem, recv_sem=rsem,
            device_id=device, device_id_type=MESH,
        )
        copy.start()
        sent.append(copy)

    def arrive(dst, ssem, rsem):
        pltpu.make_async_remote_copy(
            src_ref=dst, dst_ref=dst, send_sem=ssem, recv_sem=rsem,
            device_id=partner, device_id_type=MESH,
        ).wait_recv()

    barrier = pltpu.get_barrier_semaphore()
    for d in range(1, nc):
        pl.semaphore_signal(barrier, inc=1, device_id=to_z(d), device_id_type=MESH)
    for d in range(1, nx):
        pl.semaphore_signal(barrier, inc=1, device_id=to_x(d), device_id_type=MESH)
    pl.semaphore_signal(barrier, inc=1, device_id=partner, device_id_type=MESH)

    v_copies = [pltpu.make_async_copy(vol_hbm.at[i], vbuf.at[i], v_sem.at[i]) for i in range(ax)]
    for copy in v_copies:
        copy.start()

    for g in range(ng):
        wpack[s, c, g] = jnp.concatenate([w_ref[q * ng + g] for q in range(pk)], axis=-1)

    pl.semaphore_wait(barrier, nc - 1 + nx - 1 + 1)

    for d in range(1, nc):
        send(wpack.at[s, c], wpack.at[s, c], zs.at[d], zr.at[d], to_z(d))

    def forward_own(dz):
        shard = wpack.at[s, c_from(dz)]
        for d in range(1, nx):
            send(shard, shard, xs.at[d, dz], xr.at[d, dz], to_x(d))
        send(shard, shard, ks.at[0, dz], kr.at[0, dz], partner)

    forward_own(0)

    for t in range(nc):
        piece = cot_ref[:, t * half_j:(t + 1) * half_j].reshape(cells, oc)
        cot_out[t] = jnp.concatenate([piece[q * short:(q + 1) * short] for q in range(pk)], axis=-1)
    for d in range(1, nc):
        send(cot_out.at[c_at(d)], cot_in.at[c], ts.at[d], tr.at[d], to_z(d))
    cot_in[c] = cot_out[c]

    def split_plane(i, a):
        for j in range(half_j):
            for b in range(2):
                plane = vbuf[2 * i + a, 2 * j + b].astype(F32)
                slot = (j * 2 + b) % 2
                at = (i * half_j + j) * half_l
                for h in range(halves):
                    tmp[slot, h] = plane[:, h * LANES:(h + 1) * LANES]
                    for e in range(2):
                        k = 4 * a + 2 * b + e
                        lane = k * cin + h * LANES
                        piece = tmp[slot, h, pl.ds(e, half_l, stride=2), :].astype(BF)
                        rows[at:at + half_l, lane:lane + LANES] = piece
                        cols[lane:lane + LANES, at:at + half_l] = piece.T

    order = [(i, a) for i in range(half_i) for a in range(2)]
    for i, a in order[:2]:
        v_copies[2 * i + a].wait()
        split_plane(i, a)

    for d in range(1, nc):
        arrive(wpack.at[s, c_from(d)], zs.at[d], zr.at[d])
        forward_own(d)
    for i, a in order[2:3]:
        v_copies[2 * i + a].wait()
        split_plane(i, a)
    for dz in range(nc):
        for d in range(1, nx):
            shard = wpack.at[x_from(d) * 2 + core, c_from(dz)]
            arrive(shard, xs.at[d, dz], xr.at[d, dz])
            send(shard, shard, ks.at[d, dz], kr.at[d, dz], partner)
    for i, a in order[3:]:
        v_copies[2 * i + a].wait()
        split_plane(i, a)
    for dz in range(nc):
        for d in range(nx):
            arrive(wpack.at[x_from(d) * 2 + other, c_from(dz)], ks.at[d, dz], kr.at[d, dz])

    for g in range(ng):
        for q in range(pk):
            for t in range(ns):
                at = (q * ng + g) * cin + t * ci
                wfull[at:at + ci, :] = jnp.concatenate(
                    [wpack[t, u, g][:, q * oc:(q + 1) * oc] for u in range(nc)], axis=-1
                )

    pre_act = jnp.dot(rows[...], wfull[...], preferred_element_type=F32)
    squash = jax.nn.sigmoid(pre_act)
    slopes = squash * (1.0 + pre_act * (1.0 - squash))
    for d in range(1, nc):
        arrive(cot_in.at[c_from(d)], ts.at[d], tr.at[d])
    for q in range(pk):
        upstream = jnp.concatenate(
            [cot_in[u][:, q * oc:(q + 1) * oc] for u in range(nc)], axis=-1
        )
        own_rows = slice(q * short, (q + 1) * short)
        dlt[own_rows, :] = (upstream.astype(F32) * slopes[own_rows]).astype(BF)

    def partial(g):
        parts = []
        for q in range(pk):
            k = q * ng + g
            parts.append(jnp.dot(cols[k * cin:(k + 1) * cin, :], dlt[...], preferred_element_type=F32))
        for u in range(nc):
            packed = jnp.concatenate([m[:, u * oc:(u + 1) * oc] for m in parts], axis=-1)
            for t in range(ns):
                part[g, t // 2, t % 2, u] = packed[t * ci:(t + 1) * ci]
        for d in range(nx):
            a_out[g, d] = part[g, d, other].astype(BF)
        send(a_out.at[g], a_in.at[g], as_.at[g], ar.at[g], partner)

    def stage_b(g):
        arrive(a_in.at[g], as_.at[g], ar.at[g])
        for d in range(1, nx):
            total = part[g, x_at(d), core] + a_in[g, x_at(d)].astype(F32)
            b_out[g, d - 1] = total.astype(BF)
            send(b_out.at[g, d - 1], b_in.at[g, d - 1], bs.at[g, d], br.at[g, d], to_x(d))

    def stage_c(g):
        total = part[g, x, core] + a_in[g, x].astype(F32)
        for d in range(1, nx):
            arrive(b_in.at[g, d - 1], bs.at[g, d], br.at[g, d])
            total = total + b_in[g, d - 1].astype(F32)
        own[g] = total
        for d in range(1, nc):
            c_out[g, d - 1] = own[g, c_at(d)].astype(BF)
            send(c_out.at[g, d - 1], c_in.at[g, d - 1], cs.at[g, d], cr.at[g, d], to_z(d))

    def finish(g):
        total = own[g, c]
        for d in range(1, nc):
            arrive(c_in.at[g, d - 1], cs.at[g, d], cr.at[g, d])
            total = total + c_in[g, d - 1].astype(F32)
        total = total / cells
        for q in range(pk):
            gw_ref[q * ng + g] = total[:, q * oc:(q + 1) * oc]

    o_copies = []

    def spread(n):
        a, b = n // 2, n % 2
        both = []
        for e in range(2):
            k = 4 * a + 2 * b + e
            both.append(lax.dot_general(
                dlt[...], wfull[k * cin:(k + 1) * cin, :], (((1,), (1,)), ((), ())),
                preferred_element_type=F32,
            ))
        for i in range(half_i):
            for j in range(half_j):
                at = (i * half_j + j) * half_l
                for h in range(halves):
                    for e in range(2):
                        tmp[j % 2, h, pl.ds(e, half_l, stride=2), :] = (
                            both[e][at:at + half_l, h * LANES:(h + 1) * LANES]
                        )
                    obuf[2 * i + a, 2 * j + b, :, h * LANES:(h + 1) * LANES] = tmp[j % 2, h].astype(BF)
                put = pltpu.make_async_copy(
                    obuf.at[2 * i + a, 2 * j + b], gv_hbm.at[2 * i + a, 2 * j + b],
                    o_sem.at[2 * i + a, 2 * j + b],
                )
                put.start()
                o_copies.append(put)

    for g in range(ng):
        partial(g)
        if g >= 1:
            stage_b(g - 1)
    spread(0)
    stage_b(ng - 1)
    for g in range(ng):
        if g + 1 < 4:
            spread(g + 1)
        stage_c(g)
    for n in range(min(ng + 1, 4), 4):
        spread(n)
    for g in range(ng):
        finish(g)
    for put in o_copies:
        put.wait()
    for copy in sent:
        copy.wait_send()


def shards(ns, nc, volume, weight, cotangent):
    ax, ay, nz, cin = volume.shape
    ci, oc = weight.shape[1:]
    nx = ns // 2
    pk = LANES // oc
    ng = 8 // pk
    cells = ax * ay * nz // 8
    cout = oc * nc
    dma = pltpu.SemaphoreType.DMA
    scratch = [
        pltpu.VMEM((ax, ay, nz, cin), BF),
        pltpu.VMEM((2, cin // LANES, nz, LANES), F32),
        pltpu.VMEM((cells, 8 * cin), BF),
        pltpu.VMEM((8 * cin, cells), BF),
        pltpu.VMEM((ns, nc, ng, ci, LANES), BF),
        pltpu.VMEM((8 * cin, cout), BF),
        pltpu.VMEM((nc, cells // pk, LANES), BF),
        pltpu.VMEM((nc, cells // pk, LANES), BF),
        pltpu.VMEM((cells, cout), BF),
        pltpu.VMEM((ax, ay, nz, cin), BF),
        pltpu.VMEM((ng, nx, 2, nc, ci, LANES), F32),
        pltpu.VMEM((ng, nx, nc, ci, LANES), BF),
        pltpu.VMEM((ng, nx, nc, ci, LANES), BF),
        pltpu.VMEM((ng, nx - 1, nc, ci, LANES), BF),
        pltpu.VMEM((ng, nx - 1, nc, ci, LANES), BF),
        pltpu.VMEM((ng, nc, ci, LANES), F32),
        pltpu.VMEM((ng, nc - 1, ci, LANES), BF),
        pltpu.VMEM((ng, nc - 1, ci, LANES), BF),
        dma((ax,)), dma((ax, ay)),
        dma((nc,)), dma((nc,)),
        dma((nx, nc)), dma((nx, nc)),
        dma((nx, nc)), dma((nx, nc)),
        dma((nc,)), dma((nc,)),
        dma((ng,)), dma((ng,)),
        dma((ng, nx)), dma((ng, nx)),
        dma((ng, nc)), dma((ng, nc)),
    ]
    vmem = pl.BlockSpec(memory_space=pltpu.VMEM)
    hbm = pl.BlockSpec(memory_space=pl.ANY)
    return pl.pallas_call(
        functools.partial(kernel, ns, nc),
        out_shape=(
            jax.ShapeDtypeStruct(volume.shape, BF),
            jax.ShapeDtypeStruct((8, ci, oc), F32),
        ),
        in_specs=[hbm, vmem, vmem],
        out_specs=(hbm, vmem),
        scratch_shapes=scratch,
        compiler_params=pltpu.CompilerParams(
            collective_id=0, has_side_effects=True, vmem_limit_bytes=56 << 20
        ),
        name="conv_grads",
    )(volume, weight, cotangent)


def solution(mesh):
    return jax.shard_map(
        functools.partial(shards, mesh.shape["space"], mesh.shape["chan"]),
        mesh=mesh,
        in_specs=(
            P(("groups", "space"), "chan", None, None),
            P(None, "space", "chan"),
            P(("groups", "space"), None, None, "chan"),
        ),
        out_specs=(P(("groups", "space"), "chan", None, None), P("groups", "space", "chan")),
        check_vma=False,
    )
```

time: 126 us -> 44.6 us (0.35)
  waiting for transfers between devices: 66.1 us -> 0 us
  Pallas kernels: 0 us -> 37.9 us
  blocking collectives: 17.4 us -> 0 us
  between operations: 13.9 us -> 0.65 us
  local copies, waits for them, and re-layouts: 17.9 us -> 5.8 us
  starting transfers between devices: 5.47 us -> 0 us
  matrix products: 4.93 us -> 0 us
    reduce_scatter x1 -> x0, waiting for transfers between devices: 43.7 us -> none  [shards(): lax.psum_scatter(partial_w, 'chan', scatter_dimension=2, tiled=True)]
    pallas_call x0 -> x1, Pallas kernels: none -> 37.9 us  [shards(): pl.pallas_call(functools.partial(kernel, ns, nc), out_shape=(jax.ShapeDty...]
    all_gather x1 -> x0, blocking collectives: 17.4 us -> none  [shards(): wide_w = lax.all_gather(weight, 'chan', axis=2, tiled=True)]
    unnamed x4 -> x0, waiting for transfers between devices: 15.9 us -> none
    all_to_all x1 -> x0, starting transfers between devices: 5.38 us -> none  [shards(): lax.all_to_all(cotangent, 'chan', split_axis=1, concat_axis=3, tiled=True)]
    dot_general x3 -> x0, matrix products: 4.93 us -> none  [the longest x1 2.13 us: shards(): jnp.einsum('mkc,kco->mo', patches, whole_w, preferred_element_type=jnp.fl...]
    reshape x2 -> x0, local copies, waits for them, and re-layouts: 4.41 us -> none  [the longest x1 2.21 us: unpatch(): shaped.transpose(0, 3, 1, 4, 2, 5, 6)]
    transpose x2 -> x0, local copies, waits for them, and re-layouts: 4.3 us -> none  [the longest x1 2.16 us: unpatch(): shaped.transpose(0, 3, 1, 4, 2, 5, 6)]
  transfers between devices with their start and end apart: 4 -> 0, of which waited for: 4 -> 0; matrix products, arithmetic and copies ran while one was open for 9% -> 0% of each run, Pallas kernels for 0% -> 0%
where the time goes in v1:
time: 44.6 us; the launch traced here: 44.4 us
  Pallas kernels  37.9 us (85%)
  local copies, waits for them, and re-layouts  5.8 us (13%)
  between operations  0.65 us (1%)
    pallas_call x1, Pallas kernels, shards(): pl.pallas_call(functools.partial(kernel, ns, nc), out_shape=(jax.ShapeDty...  37.9 us
    unnamed x5, local copies, waits for them, and re-layouts  5.8 us

profile of v1, /device:TPU:0, one launch (start us, length us, event | category | flops | bytes accessed | tf_op | source)
XLA Modules:
  0.0 44.4 jit_solution(11769534070427194036)
XLA Ops:
  0.6 2.0 %copy.5.cot_ref = bf16[2,8,128,64]{3,2,1,0:T(8,128)(2,1)} copy(bf16[2,8,128,64]{2,3,1,0:T(8,128)(2,1)} %param.5) | data formatting | bytes 524288 | tf_op args[2]
  2.6 37.9 %conv_grads.1 = (bf16[4,4,256,256]{3,2,1,0:T(8,128)(2,1)}, f32[8,64,64]{2,1,0:T(8,128)}) custom-call(bf16[4,4,256,256]{3,2,1,0:T(8,128)(2,1)} %vol_hbm.1, bf16[8,64,64]{2,1,0:T(8,128)(2,1)} %w_ref.1, bf16[2,8,128,64]{3,2,1,0:T(8,128)(2,1)} %copy.5.cot_ref), custom_call_target="tpu_custom_call" | custom-call | tf_op jit(solution)/shard_map/conv_grads/pallas_call | solution.py:288
  40.5 0.0 copy-start
  40.5 3.1 %copy.8 = bf16[4,4,256,256]{3,2,1,0:T(8,128)(2,1)} copy(bf16[4,4,256,256]{3,2,1,0:T(8,128)(2,1)} %get-tuple-element.4) | data formatting | bytes 4194304
  43.7 0.0 copy-done
  43.7 0.7 %copy.9 = f32[8,64,64]{2,1,0:T(8,128)} copy(f32[8,64,64]{2,1,0:T(8,128)S(1)} %copy-done) | data formatting | bytes 262144
Async XLA Ops:
  40.5 3.1 %copy-start = (f32[8,64,64]{2,1,0:T(8,128)S(1)}, f32[8,64,64]{2,1,0:T(8,128)}, u32[]{:S(2)}) copy-start(f32[8,64,64]{2,1,0:T(8,128)} %get-tuple-element.5) | copy-start | bytes 393220

commit v2 on v1

--- a/solution.py
+++ b/solution.py
@@ -14,10 +14,10 @@
 
 
 def kernel(
-    ns, nc, vol_hbm, w_ref, cot_ref, gv_hbm, gw_ref,
-    vbuf, tmp, rows, cols, wpack, wfull, cot_out, cot_in, dlt, obuf,
+    ns, nc, vol_hbm, w_hbm, cot_hbm, obuf, gw_ref,
+    w_ref, vbuf, tmp, rows, cols, wpack, wfull, cot_in, dlt,
     part, a_out, a_in, b_out, b_in, own, c_out, c_in,
-    v_sem, o_sem, zs, zr, xs, xr, ks, kr, ts, tr, as_, ar, bs, br, cs, cr,
+    w_sem, v_sem, t_sem, zs, zr, xs, xr, ks, kr, ts, tr, as_, ar, bs, br, cs, cr,
 ):
     nx = ns // 2
     ax, ay, nz, cin = vbuf.shape
@@ -26,7 +26,6 @@
     ng = 8 // pk
     half_i, half_j, half_l = ax // 2, ay // 2, nz // 2
     cells = half_i * half_j * half_l
-    short = cells // pk
     halves = cin // LANES
 
     s, c = lax.axis_index("space"), lax.axis_index("chan")
@@ -61,6 +60,7 @@
         )
         copy.start()
         sent.append(copy)
+        return copy
 
     def arrive(dst, ssem, rsem):
         pltpu.make_async_remote_copy(
@@ -68,6 +68,8 @@
             device_id=partner, device_id_type=MESH,
         ).wait_recv()
 
+    w_copy = pltpu.make_async_copy(w_hbm, w_ref, w_sem)
+    w_copy.start()
     barrier = pltpu.get_barrier_semaphore()
     for d in range(1, nc):
         pl.semaphore_signal(barrier, inc=1, device_id=to_z(d), device_id_type=MESH)
@@ -79,13 +81,14 @@
     for copy in v_copies:
         copy.start()
 
+    w_copy.wait()
     for g in range(ng):
         wpack[s, c, g] = jnp.concatenate([w_ref[q * ng + g] for q in range(pk)], axis=-1)
 
     pl.semaphore_wait(barrier, nc - 1 + nx - 1 + 1)
 
-    for d in range(1, nc):
-        send(wpack.at[s, c], wpack.at[s, c], zs.at[d], zr.at[d], to_z(d))
+    near = sorted(range(1, nc), key=lambda d: (min(d, nc - d), d))
+    first = [send(wpack.at[s, c], wpack.at[s, c], zs.at[d], zr.at[d], to_z(d)) for d in near]
 
     def forward_own(dz):
         shard = wpack.at[s, c_from(dz)]
@@ -95,12 +98,11 @@
 
     forward_own(0)
 
-    for t in range(nc):
-        piece = cot_ref[:, t * half_j:(t + 1) * half_j].reshape(cells, oc)
-        cot_out[t] = jnp.concatenate([piece[q * short:(q + 1) * short] for q in range(pk)], axis=-1)
-    for d in range(1, nc):
-        send(cot_out.at[c_at(d)], cot_in.at[c], ts.at[d], tr.at[d], to_z(d))
-    cot_in[c] = cot_out[c]
+    def cot_piece(d):
+        return cot_hbm.at[:, pl.ds(c_at(d) * half_j, half_j)]
+
+    cot_own = pltpu.make_async_copy(cot_piece(0), cot_in.at[c], t_sem)
+    cot_own.start()
 
     def split_plane(i, a):
         for j in range(half_j):
@@ -122,7 +124,13 @@
         v_copies[2 * i + a].wait()
         split_plane(i, a)
 
-    for d in range(1, nc):
+    for n, d in enumerate(near):
+        if n == len(near) - 1:
+            for copy in first:
+                copy.wait_send()
+                sent.remove(copy)
+            for t in near:
+                send(cot_piece(t), cot_in.at[c], ts.at[t], tr.at[t], to_z(t))
         arrive(wpack.at[s, c_from(d)], zs.at[d], zr.at[d])
         forward_own(d)
     for i, a in order[2:3]:
@@ -151,14 +159,14 @@
     pre_act = jnp.dot(rows[...], wfull[...], preferred_element_type=F32)
     squash = jax.nn.sigmoid(pre_act)
     slopes = squash * (1.0 + pre_act * (1.0 - squash))
-    for d in range(1, nc):
+    cot_own.wait()
+    for d in near:
         arrive(cot_in.at[c_from(d)], ts.at[d], tr.at[d])
-    for q in range(pk):
-        upstream = jnp.concatenate(
-            [cot_in[u][:, q * oc:(q + 1) * oc] for u in range(nc)], axis=-1
-        )
-        own_rows = slice(q * short, (q + 1) * short)
-        dlt[own_rows, :] = (upstream.astype(F32) * slopes[own_rows]).astype(BF)
+    for i in range(half_i):
+        for j in range(half_j):
+            at = (i * half_j + j) * half_l
+            upstream = jnp.concatenate([cot_in[u, i, j] for u in range(nc)], axis=0).T
+            dlt[at:at + half_l, :] = (upstream.astype(F32) * slopes[at:at + half_l]).astype(BF)
 
     def partial(g):
         parts = []
@@ -198,8 +206,6 @@
         total = total / cells
         for q in range(pk):
             gw_ref[q * ng + g] = total[:, q * oc:(q + 1) * oc]
-
-    o_copies = []
 
     def spread(n):
         a, b = n // 2, n % 2
@@ -219,12 +225,6 @@
                             both[e][at:at + half_l, h * LANES:(h + 1) * LANES]
                         )
                     obuf[2 * i + a, 2 * j + b, :, h * LANES:(h + 1) * LANES] = tmp[j % 2, h].astype(BF)
-                put = pltpu.make_async_copy(
-                    obuf.at[2 * i + a, 2 * j + b], gv_hbm.at[2 * i + a, 2 * j + b],
-                    o_sem.at[2 * i + a, 2 * j + b],
-                )
-                put.start()
-                o_copies.append(put)
 
     for g in range(ng):
         partial(g)
@@ -240,10 +240,19 @@
         spread(n)
     for g in range(ng):
         finish(g)
-    for put in o_copies:
-        put.wait()
     for copy in sent:
         copy.wait_send()
+
+
+def place(gv_ref, gw_ref, gv_hbm, gw_hbm, sem):
+    puts = [
+        pltpu.make_async_copy(gv_ref, gv_hbm, sem.at[0]),
+        pltpu.make_async_copy(gw_ref, gw_hbm, sem.at[1]),
+    ]
+    for put in puts:
+        put.start()
+    for put in puts:
+        put.wait()
 
 
 def shards(ns, nc, volume, weight, cotangent):
@@ -256,16 +265,15 @@
     cout = oc * nc
     dma = pltpu.SemaphoreType.DMA
     scratch = [
+        pltpu.VMEM((8, ci, oc), BF),
         pltpu.VMEM((ax, ay, nz, cin), BF),
         pltpu.VMEM((2, cin // LANES, nz, LANES), F32),
         pltpu.VMEM((cells, 8 * cin), BF),
         pltpu.VMEM((8 * cin, cells), BF),
         pltpu.VMEM((ns, nc, ng, ci, LANES), BF),
         pltpu.VMEM((8 * cin, cout), BF),
-        pltpu.VMEM((nc, cells // pk, LANES), BF),
-        pltpu.VMEM((nc, cells // pk, LANES), BF),
+        pltpu.VMEM((nc, ax // 2, ay // 2, oc, nz // 2), BF),
         pltpu.VMEM((cells, cout), BF),
-        pltpu.VMEM((ax, ay, nz, cin), BF),
         pltpu.VMEM((ng, nx, 2, nc, ci, LANES), F32),
         pltpu.VMEM((ng, nx, nc, ci, LANES), BF),
         pltpu.VMEM((ng, nx, nc, ci, LANES), BF),
@@ -274,7 +282,7 @@
         pltpu.VMEM((ng, nc, ci, LANES), F32),
         pltpu.VMEM((ng, nc - 1, ci, LANES), BF),
         pltpu.VMEM((ng, nc - 1, ci, LANES), BF),
-        dma((ax,)), dma((ax, ay)),
+        dma(()), dma((ax,)), dma(()),
         dma((nc,)), dma((nc,)),
         dma((nx, nc)), dma((nx, nc)),
         dma((nx, nc)), dma((nx, nc)),
@@ -284,21 +292,33 @@
         dma((ng, nc)), dma((ng, nc)),
     ]
     vmem = pl.BlockSpec(memory_space=pltpu.VMEM)
-    hbm = pl.BlockSpec(memory_space=pl.ANY)
-    return pl.pallas_call(
+    hbm = pl.BlockSpec(memory_space=pltpu.HBM)
+    sums = pl.pallas_call(
         functools.partial(kernel, ns, nc),
         out_shape=(
             jax.ShapeDtypeStruct(volume.shape, BF),
             jax.ShapeDtypeStruct((8, ci, oc), F32),
         ),
-        in_specs=[hbm, vmem, vmem],
-        out_specs=(hbm, vmem),
+        in_specs=[hbm, hbm, hbm],
+        out_specs=(vmem, vmem),
         scratch_shapes=scratch,
         compiler_params=pltpu.CompilerParams(
-            collective_id=0, has_side_effects=True, vmem_limit_bytes=56 << 20
+            collective_id=0, has_side_effects=True, vmem_limit_bytes=32 << 20
         ),
         name="conv_grads",
-    )(volume, weight, cotangent)
+    )(*(pltpu.with_memory_space_constraint(v, pltpu.HBM) for v in (volume, weight, cotangent.transpose(0, 1, 3, 2))))
+    return pl.pallas_call(
+        place,
+        out_shape=(
+            jax.ShapeDtypeStruct(volume.shape, BF),
+            jax.ShapeDtypeStruct((8, ci, oc), F32),
+        ),
+        in_specs=[vmem, vmem],
+        out_specs=(hbm, hbm),
+        scratch_shapes=[dma((2,))],
+        compiler_params=pltpu.CompilerParams(vmem_limit_bytes=8 << 20),
+        name="place",
+    )(*sums)
 
 
 def solution(mesh):

time: 44.6 us -> 35.7 us (0.80)
  local copies, waits for them, and re-layouts: 5.8 us -> 0 us
  Pallas kernels: 37.9 us -> 34.9 us
    unnamed x5 -> x0, local copies, waits for them, and re-layouts: 5.8 us -> none
    pallas_call x1, Pallas kernels: 37.9 us -> 33.5 us  [shards(): pl.pallas_call(functools.partial(kernel, ns, nc), out_shape=(jax.ShapeDty...]
    pallas_call x0 -> x1, Pallas kernels: none -> 1.41 us  [shards(): pl.pallas_call(place, out_shape=(jax.ShapeDtypeStruct(volume.shape, BF),...]
where the time goes in v2:
time: 35.7 us; the launch traced here: 35.6 us
  Pallas kernels  34.9 us (98%)
  between operations  0.64 us (2%)
    pallas_call x1, Pallas kernels, shards(): pl.pallas_call(functools.partial(kernel, ns, nc), out_shape=(jax.ShapeDty...  33.5 us
    pallas_call x1, Pallas kernels, shards(): pl.pallas_call(place, out_shape=(jax.ShapeDtypeStruct(volume.shape, BF),...  1.41 us

profile of v2, /device:TPU:0, one launch (start us, length us, event | category | flops | bytes accessed | tf_op | source)
XLA Modules:
  0.0 35.6 jit_solution(4088685711653544192)
XLA Ops:
  0.6 33.5 %conv_grads.1 = (bf16[4,4,256,256]{3,2,1,0:T(8,128)(2,1)S(1)}, f32[8,64,64]{2,1,0:T(8,128)S(1)}) custom-call(bf16[4,4,256,256]{3,2,1,0:T(8,128)(2,1)} %vol_hbm.1, bf16[8,64,64]{2,1,0:T(8,128)(2,1)} %w_hbm.1, bf16[2,8,64,128]{3,2,1,0:T(8,128)(2,1)} %bitcast.1), custom_call_target="tpu_custom_call" | custom-call | tf_op jit(solution)/shard_map/conv_grads/pallas_call | solution.py:296
  34.2 1.4 %place.1 = (bf16[4,4,256,256]{3,2,1,0:T(8,128)(2,1)}, f32[8,64,64]{2,1,0:T(8,128)}) custom-call(bf16[4,4,256,256]{3,2,1,0:T(8,128)(2,1)S(1)} %get-tuple-element.4.gv_ref, f32[8,64,64]{2,1,0:T(8,128)S(1)} %get-tuple-element.5.gw_ref), custom_call_target="tpu_custom_call" | custom-call | tf_op jit(solution)/shard_map/place/pallas_call | solution.py:310

commit v3 on v2

--- a/solution.py
+++ b/solution.py
@@ -17,6 +17,7 @@
     ns, nc, vol_hbm, w_hbm, cot_hbm, obuf, gw_ref,
     w_ref, vbuf, tmp, rows, cols, wpack, wfull, cot_in, dlt,
     part, a_out, a_in, b_out, b_in, own, c_out, c_in,
+    e_out, e_in, f_out, f_in, held,
     w_sem, v_sem, t_sem, zs, zr, xs, xr, ks, kr, ts, tr, as_, ar, bs, br, cs, cr,
 ):
     nx = ns // 2
@@ -88,15 +89,36 @@
     pl.semaphore_wait(barrier, nc - 1 + nx - 1 + 1)
 
     near = sorted(range(1, nc), key=lambda d: (min(d, nc - d), d))
-    first = [send(wpack.at[s, c], wpack.at[s, c], zs.at[d], zr.at[d], to_z(d)) for d in near]
-
-    def forward_own(dz):
-        shard = wpack.at[s, c_from(dz)]
+    hz = ng
+    spans = [pl.ds(0, hz)] + ([pl.ds(hz, ng - hz)] if ng > hz else [])
+
+    def shard(m, dx, dz, n):
+        return wpack.at[x_from(dx) * 2 + m, c_from(dz), spans[n]]
+
+    def pass_x(n, dz):
         for d in range(1, nx):
-            send(shard, shard, xs.at[d, dz], xr.at[d, dz], to_x(d))
-        send(shard, shard, ks.at[0, dz], kr.at[0, dz], partner)
-
-    forward_own(0)
+            send(shard(core, 0, dz, n), shard(core, 0, dz, n), xs.at[n, d, dz], xr.at[n, d, dz], to_x(d))
+
+    def pass_z(n, dx):
+        for d in near:
+            send(shard(core, dx, 0, n), shard(core, dx, 0, n), zs.at[n, dx, d], zr.at[n, dx, d], to_z(d))
+
+    def pass_core(n, dx, dz):
+        send(shard(core, dx, dz, n), shard(core, dx, dz, n), ks.at[n, dx, dz], kr.at[n, dx, dz], partner)
+
+    def from_x(n, dx, dz):
+        arrive(shard(core, dx, dz, n), xs.at[n, dx, dz], xr.at[n, dx, dz])
+
+    def from_z(n, dx, dz):
+        arrive(shard(core, dx, dz, n), zs.at[n, dx, dz], zr.at[n, dx, dz])
+
+    for n in range(len(spans)):
+        pass_z(n, 0)
+    first = list(sent)
+    for n in reversed(range(len(spans))):
+        pass_x(n, 0)
+    for n in range(len(spans)):
+        pass_core(n, 0, 0)
 
     def cot_piece(d):
         return cot_hbm.at[:, pl.ds(c_at(d) * half_j, half_j)]
@@ -124,29 +146,41 @@
         v_copies[2 * i + a].wait()
         split_plane(i, a)
 
-    for n, d in enumerate(near):
-        if n == len(near) - 1:
+    if len(spans) > 1:
+        for dx in range(1, nx):
+            from_x(1, dx, 0)
+            pass_z(1, dx)
+            pass_core(1, dx, 0)
+    for dz in near:
+        if dz == near[-1]:
             for copy in first:
                 copy.wait_send()
                 sent.remove(copy)
             for t in near:
                 send(cot_piece(t), cot_in.at[c], ts.at[t], tr.at[t], to_z(t))
-        arrive(wpack.at[s, c_from(d)], zs.at[d], zr.at[d])
-        forward_own(d)
+        from_z(0, 0, dz)
+        pass_x(0, dz)
+        pass_core(0, 0, dz)
     for i, a in order[2:3]:
         v_copies[2 * i + a].wait()
         split_plane(i, a)
-    for dz in range(nc):
-        for d in range(1, nx):
-            shard = wpack.at[x_from(d) * 2 + core, c_from(dz)]
-            arrive(shard, xs.at[d, dz], xr.at[d, dz])
-            send(shard, shard, ks.at[d, dz], kr.at[d, dz], partner)
+    for dz in [0] + near:
+        if len(spans) > 1 and dz > 0:
+            from_z(1, 0, dz)
+            pass_core(1, 0, dz)
+        for dx in range(1, nx):
+            from_x(0, dx, dz)
+            pass_core(0, dx, dz)
+            if len(spans) > 1 and dz > 0:
+                from_z(1, dx, dz)
+                pass_core(1, dx, dz)
     for i, a in order[3:]:
         v_copies[2 * i + a].wait()
         split_plane(i, a)
-    for dz in range(nc):
-        for d in range(nx):
-            arrive(wpack.at[x_from(d) * 2 + other, c_from(dz)], ks.at[d, dz], kr.at[d, dz])
+    for dz in [0] + near:
+        for dx in range(nx):
+            for n in range(len(spans)):
+                arrive(shard(other, dx, dz, n), ks.at[n, dx, dz], kr.at[n, dx, dz])
 
     for g in range(ng):
         for q in range(pk):
@@ -181,28 +215,54 @@
             a_out[g, d] = part[g, d, other].astype(BF)
         send(a_out.at[g], a_in.at[g], as_.at[g], ar.at[g], partner)
 
+    def half_sum(g, t, u):
+        return part[g, t, core, u] + a_in[g, t, u].astype(F32)
+
     def stage_b(g):
         arrive(a_in.at[g], as_.at[g], ar.at[g])
-        for d in range(1, nx):
-            total = part[g, x_at(d), core] + a_in[g, x_at(d)].astype(F32)
-            b_out[g, d - 1] = total.astype(BF)
-            send(b_out.at[g, d - 1], b_in.at[g, d - 1], bs.at[g, d], br.at[g, d], to_x(d))
+        if g % 2 == 0:
+            for d in range(1, nx):
+                total = part[g, x_at(d), core] + a_in[g, x_at(d)].astype(F32)
+                b_out[g, d - 1] = total.astype(BF)
+                send(b_out.at[g, d - 1], b_in.at[g, d - 1], bs.at[g, d], br.at[g, d], to_x(d))
+        else:
+            for d in near:
+                for t in range(nx):
+                    e_out[g, d - 1, t] = half_sum(g, t, c_at(d)).astype(BF)
+                send(e_out.at[g, d - 1], e_in.at[g, d - 1], cs.at[g, d], cr.at[g, d], to_z(d))
 
     def stage_c(g):
-        total = part[g, x, core] + a_in[g, x].astype(F32)
-        for d in range(1, nx):
-            arrive(b_in.at[g, d - 1], bs.at[g, d], br.at[g, d])
-            total = total + b_in[g, d - 1].astype(F32)
-        own[g] = total
-        for d in range(1, nc):
-            c_out[g, d - 1] = own[g, c_at(d)].astype(BF)
-            send(c_out.at[g, d - 1], c_in.at[g, d - 1], cs.at[g, d], cr.at[g, d], to_z(d))
+        if g % 2 == 0:
+            total = part[g, x, core] + a_in[g, x].astype(F32)
+            for d in range(1, nx):
+                arrive(b_in.at[g, d - 1], bs.at[g, d], br.at[g, d])
+                total = total + b_in[g, d - 1].astype(F32)
+            own[g] = total
+            for d in near:
+                c_out[g, d - 1] = own[g, c_at(d)].astype(BF)
+                send(c_out.at[g, d - 1], c_in.at[g, d - 1], cs.at[g, d], cr.at[g, d], to_z(d))
+        else:
+            totals = [half_sum(g, t, c) for t in range(nx)]
+            for d in near:
+                arrive(e_in.at[g, d - 1], cs.at[g, d], cr.at[g, d])
+                totals = [totals[t] + e_in[g, d - 1, t].astype(F32) for t in range(nx)]
+            for t in range(nx):
+                held[g, t] = totals[t]
+            for d in range(1, nx):
+                f_out[g, d - 1] = held[g, x_at(d)].astype(BF)
+                send(f_out.at[g, d - 1], f_in.at[g, d - 1], bs.at[g, d], br.at[g, d], to_x(d))
 
     def finish(g):
-        total = own[g, c]
-        for d in range(1, nc):
-            arrive(c_in.at[g, d - 1], cs.at[g, d], cr.at[g, d])
-            total = total + c_in[g, d - 1].astype(F32)
+        if g % 2 == 0:
+            total = own[g, c]
+            for d in near:
+                arrive(c_in.at[g, d - 1], cs.at[g, d], cr.at[g, d])
+                total = total + c_in[g, d - 1].astype(F32)
+        else:
+            total = held[g, x]
+            for d in range(1, nx):
+                arrive(f_in.at[g, d - 1], bs.at[g, d], br.at[g, d])
+                total = total + f_in[g, d - 1].astype(F32)
         total = total / cells
         for q in range(pk):
             gw_ref[q * ng + g] = total[:, q * oc:(q + 1) * oc]
@@ -282,10 +342,15 @@
         pltpu.VMEM((ng, nc, ci, LANES), F32),
         pltpu.VMEM((ng, nc - 1, ci, LANES), BF),
         pltpu.VMEM((ng, nc - 1, ci, LANES), BF),
+        pltpu.VMEM((ng, nc - 1, nx, ci, LANES), BF),
+        pltpu.VMEM((ng, nc - 1, nx, ci, LANES), BF),
+        pltpu.VMEM((ng, nx - 1, ci, LANES), BF),
+        pltpu.VMEM((ng, nx - 1, ci, LANES), BF),
+        pltpu.VMEM((ng, nx, ci, LANES), F32),
         dma(()), dma((ax,)), dma(()),
-        dma((nc,)), dma((nc,)),
-        dma((nx, nc)), dma((nx, nc)),
-        dma((nx, nc)), dma((nx, nc)),
+        dma((2, nx, nc)), dma((2, nx, nc)),
+        dma((2, nx, nc)), dma((2, nx, nc)),
+        dma((2, nx, nc)), dma((2, nx, nc)),
         dma((nc,)), dma((nc,)),
         dma((ng,)), dma((ng,)),
         dma((ng, nx)), dma((ng, nx)),

time: 35.7 us -> 34.6 us (0.969)
  Pallas kernels: 34.9 us -> 33.8 us
    pallas_call x1, Pallas kernels: 33.5 us -> 32.4 us  [shards(): pl.pallas_call(functools.partial(kernel, ns, nc), out_shape=(jax.ShapeDty...]
where the time goes in v3:
time: 34.6 us; the launch traced here: 34.4 us
  Pallas kernels  33.8 us (98%)
  between operations  0.64 us (2%)
    pallas_call x1, Pallas kernels, shards(): pl.pallas_call(functools.partial(kernel, ns, nc), out_shape=(jax.ShapeDty...  32.4 us
    pallas_call x1, Pallas kernels, shards(): pl.pallas_call(place, out_shape=(jax.ShapeDtypeStruct(volume.shape, BF),...  1.41 us

profile of v3, /device:TPU:0, one launch (start us, length us, event | category | flops | bytes accessed | tf_op | source)
XLA Modules:
  0.0 34.4 jit_solution(10362606484430041367)
XLA Ops:
  0.6 32.4 %conv_grads.1 = (bf16[4,4,256,256]{3,2,1,0:T(8,128)(2,1)S(1)}, f32[8,64,64]{2,1,0:T(8,128)S(1)}) custom-call(bf16[4,4,256,256]{3,2,1,0:T(8,128)(2,1)} %vol_hbm.1, bf16[8,64,64]{2,1,0:T(8,128)(2,1)} %w_hbm.1, bf16[2,8,64,128]{3,2,1,0:T(8,128)(2,1)} %bitcast.1), custom_call_target="tpu_custom_call" | custom-call | tf_op jit(solution)/shard_map/conv_grads/pallas_call | solution.py:361
  33.0 1.4 %place.1 = (bf16[4,4,256,256]{3,2,1,0:T(8,128)(2,1)}, f32[8,64,64]{2,1,0:T(8,128)}) custom-call(bf16[4,4,256,256]{3,2,1,0:T(8,128)(2,1)S(1)} %get-tuple-element.4.gv_ref, f32[8,64,64]{2,1,0:T(8,128)S(1)} %get-tuple-element.5.gw_ref), custom_call_target="tpu_custom_call" | custom-call | tf_op jit(solution)/shard_map/place/pallas_call | solution.py:375
